TPU v7x, 32 devices: a whole 2x2x4 slice. The times are simulated.
32 devices in a mesh: groups: 2 (over x), fsdp: 16 (over z, y, core).
Axes of the slice: x: 2, y: 2, z: 4, core: 2. Of those that a mesh axis runs over, the one named last changes fastest.
Arguments:
- layer_input: bfloat16 [512, 8192], P('groups', 'fsdp'), parts along dimension 0, may hold values from -6 to 6
- norm_gain: bfloat16 [8192], P('fsdp'), may hold values from 0.099609375 to 1.8984375
- w_query: bfloat16 [8192, 8192], P(None, 'fsdp'), may hold values from -0.0625 to 0.0625
- w_key: bfloat16 [8192, 1024], P('fsdp'), may hold values from -0.09375 to 0.09375
- w_value: bfloat16 [8192, 1024], P('fsdp'), may hold values from -0.09375 to 0.09375
- w_out: bfloat16 [8192, 8192], P('fsdp'), may hold values from -0.0625 to 0.0625
- cart_key: bfloat16 [4096, 1024], P(('groups', 'fsdp')), parts along dimension 0, may hold values from -100 to 100
- cart_value: bfloat16 [4096, 1024], P(('groups', 'fsdp')), parts along dimension 0, may hold values from -6 to 6
- grad_out: bfloat16 [512, 8192], P('groups', 'fsdp'), parts along dimension 0, may hold values from -6 to 6
Outputs:
- attn_out: bfloat16 [512, 8192], P('groups', 'fsdp'), parts along dimension 0
- grad_key: float32 [4096, 1024], P(('groups', 'fsdp')), parts along dimension 0
- grad_value: float32 [4096, 1024], P(('groups', 'fsdp')), parts along dimension 0
- new_keys: bfloat16 [512, 1024], P('groups', 'fsdp'), parts along dimension 0
- new_values: bfloat16 [512, 1024], P('groups', 'fsdp'), parts along dimension 0
There are 2 independent parts, one for each index of `groups`. A program takes and returns all parts, laid end to end along the dimension named above; an argument that names none is the same for every part. Nothing has to cross between parts.
All inputs are finite; a program needn't handle non-finite values.
Results may differ from a plain program's by a relative error of at most 0.015.
The roundings to bfloat16 on the way count: a program that leaves them out, or rounds other values in their place, can miss the bound.
Values may be sent and summed in bfloat16 or wider, within the bound.
A program may use at most 128 MiB of HBM per device.

v0:
```python
import jax
import jax.numpy as jnp
from jax import lax
from jax.sharding import PartitionSpec as P

H = 64
KV = 8
HD = 128
C = 2048
SEQ = 64


def rotate(vectors, positions):
    half_dim = vectors.shape[-1] // 2
    frequency = jnp.exp(
        -jnp.log(500000.0) * jnp.arange(half_dim, dtype=jnp.float32) * (2.0 / vectors.shape[-1])
    )
    angles = positions.astype(jnp.float32)[:, None] * frequency[None, :]
    cosines = jnp.cos(angles)[:, None, :]
    sine_table = jnp.sin(angles)[:, None, :]
    first_half = vectors[..., :half_dim]
    second = vectors[..., half_dim:]
    return jnp.concatenate(
        [first_half * cosines - second * sine_table, second * cosines + first_half * sine_table], -1
    )


def head_block(queries, slot_keys, slot_values, token_keys, token_values, grad_heads, seq_len):
    scaling = queries.shape[-1] ** (-0.5)
    token_count = queries.shape[1]
    score_cart = (
        jnp.einsum("gtd,cd->gtc", queries, slot_keys, preferred_element_type=jnp.float32) * scaling
    )
    score_tok = (
        jnp.einsum("gtd,sd->gts", queries, token_keys, preferred_element_type=jnp.float32) * scaling
    )
    index_rows = jnp.arange(token_count)
    causal = (index_rows[:, None] // seq_len == index_rows[None, :] // seq_len) & (
        index_rows[None, :] <= index_rows[:, None]
    )
    score_tok = jnp.where(causal[None], score_tok, -jnp.inf)
    row_max = jnp.maximum(
        jnp.max(score_cart, -1, keepdims=True), jnp.max(score_tok, -1, keepdims=True)
    )
    exp_cart = jnp.exp(score_cart - row_max)
    exp_tok = jnp.exp(score_tok - row_max)
    totals = jnp.sum(exp_cart, -1, keepdims=True) + jnp.sum(exp_tok, -1, keepdims=True)
    prob_cart = exp_cart / totals
    rounded_cart = prob_cart.astype(jnp.bfloat16)
    rounded_tok = (exp_tok / totals).astype(jnp.bfloat16)
    mixture = jnp.einsum(
        "gtc,cd->gtd", rounded_cart, slot_values, preferred_element_type=jnp.float32
    )
    mixture = mixture + jnp.einsum(
        "gts,sd->gtd", rounded_tok, token_values, preferred_element_type=jnp.float32
    )
    outputs = mixture.astype(jnp.bfloat16)
    grad_prob_cart = jnp.einsum(
        "gtd,cd->gtc", grad_heads, slot_values, preferred_element_type=jnp.float32
    )
    deltas = jnp.sum(
        grad_heads.astype(jnp.float32) * outputs.astype(jnp.float32), -1, keepdims=True
    )
    grad_score = (prob_cart * (grad_prob_cart - deltas)).astype(jnp.bfloat16)
    grad_keys = (
        jnp.einsum("gtc,gtd->cd", grad_score, queries, preferred_element_type=jnp.float32) * scaling
    )
    grad_values = jnp.einsum(
        "gtc,gtd->cd", rounded_cart, grad_heads, preferred_element_type=jnp.float32
    )
    return (outputs, grad_keys, grad_values)


def on_device(
    layer_input, norm_gain, w_query, w_key, w_value, w_out, cart_key, cart_value, grad_out
):
    devices = lax.axis_size("fsdp")
    my_index = lax.axis_index("fsdp")
    token_count = layer_input.shape[0]
    feature_count = layer_input.shape[1]
    local_heads = w_query.shape[1] // HD
    slot_count = cart_key.shape[0]
    kv_width = w_key.shape[1]
    gathered, gathered_gain = (
        lax.all_gather(layer_input, "fsdp", axis=1, tiled=True),
        lax.all_gather(norm_gain, "fsdp", axis=0, tiled=True),
    )
    gathered_f32 = gathered.astype(jnp.float32)
    inverse_rms = lax.rsqrt(jnp.mean(gathered_f32 * gathered_f32, -1, keepdims=True) + 1e-05)
    normed = (gathered_f32 * inverse_rms * gathered_gain.astype(jnp.float32)[None, :]).astype(
        jnp.bfloat16
    )
    own_part = lax.dynamic_slice_in_dim(normed, my_index * feature_count, feature_count, 1)
    partial_kv = jnp.concatenate(
        [
            jnp.dot(own_part, w_key, preferred_element_type=jnp.float32),
            jnp.dot(own_part, w_value, preferred_element_type=jnp.float32),
        ],
        1,
    )
    token_kv = lax.psum(partial_kv, "fsdp")
    positions = C + jnp.arange(token_count) % SEQ
    all_token_keys = (
        rotate(token_kv[:, :kv_width].reshape(token_count, kv_width // HD, HD), positions)
        .reshape(token_count, kv_width)
        .astype(jnp.bfloat16)
    )
    all_token_values = token_kv[:, kv_width:].astype(jnp.bfloat16)
    column_count = kv_width // devices
    new_keys = lax.dynamic_slice_in_dim(all_token_keys, my_index * column_count, column_count, 1)
    new_values = lax.dynamic_slice_in_dim(
        all_token_values, my_index * column_count, column_count, 1
    )
    kv_group = my_index * local_heads // (H // KV)
    token_keys = lax.dynamic_slice_in_dim(all_token_keys, kv_group * HD, HD, 1)
    token_values = lax.dynamic_slice_in_dim(all_token_values, kv_group * HD, HD, 1)
    queries = jnp.dot(normed, w_query, preferred_element_type=jnp.float32).reshape(
        token_count, local_heads, HD
    )
    queries = rotate(queries, positions).astype(jnp.bfloat16).transpose(1, 0, 2)
    spread_keys = jnp.repeat(cart_key.reshape(slot_count, KV, HD), devices // KV, axis=1)
    spread_values = jnp.repeat(cart_value.reshape(slot_count, KV, HD), devices // KV, axis=1)
    own_slots = lax.all_to_all(
        jnp.concatenate([spread_keys, spread_values], 2),
        "fsdp",
        split_axis=1,
        concat_axis=0,
        tiled=True,
    )
    slot_keys = own_slots[:, 0, :HD]
    slot_values = own_slots[:, 0, HD:]
    cotangent = lax.all_gather(grad_out, "fsdp", axis=1, tiled=True)
    grad_heads = lax.dot_general(
        cotangent, w_out, (((1,), (1,)), ((), ())), preferred_element_type=jnp.float32
    )
    grad_heads = (
        grad_heads.astype(jnp.bfloat16).reshape(token_count, local_heads, HD).transpose(1, 0, 2)
    )
    outputs, grad_keys, grad_values = head_block(
        queries, slot_keys, slot_values, token_keys, token_values, grad_heads, SEQ
    )
    head_outputs = outputs.transpose(1, 0, 2).reshape(token_count, local_heads * HD)
    partial_out = jnp.dot(head_outputs, w_out, preferred_element_type=jnp.float32)
    attn_out = lax.psum_scatter(partial_out, "fsdp", scatter_dimension=1, tiled=True).astype(
        jnp.bfloat16
    )
    total_slots = grad_keys.shape[0]
    stacked = jnp.concatenate([grad_keys, grad_values], 1).reshape(
        devices, total_slots // devices, 2 * HD
    )
    received = lax.all_to_all(stacked, "fsdp", split_axis=0, concat_axis=0, tiled=True)
    summed = jnp.sum(
        received.reshape(KV, devices // KV, total_slots // devices, 2 * HD), axis=1
    ).transpose(1, 0, 2)
    grad_key = summed[:, :, :HD].reshape(total_slots // devices, KV * HD)
    grad_value = summed[:, :, HD:].reshape(total_slots // devices, KV * HD)
    return (attn_out, grad_key, grad_value, new_keys, new_values)


def solution(mesh):
    return jax.shard_map(
        on_device,
        mesh=mesh,
        in_specs=(
            P("groups", "fsdp"),
            P("fsdp"),
            P(None, "fsdp"),
            P("fsdp", None),
            P("fsdp", None),
            P("fsdp", None),
            P(("groups", "fsdp"), None),
            P(("groups", "fsdp"), None),
            P("groups", "fsdp"),
        ),
        out_specs=(
            P("groups", "fsdp"),
            P(("groups", "fsdp"), None),
            P(("groups", "fsdp"), None),
            P("groups", "fsdp"),
            P("groups", "fsdp"),
        ),
        check_vma=False,
    )
```

profile of v0, /device:TPU:0, one launch (start us, length us, event | category | flops | bytes accessed | tf_op | source)
XLA Modules:
  0.0 399.3 jit_solution(2381138714927701704)
XLA Ops:
  7.2 0.7 all-gather.4.cloned.1.call-update
  8.0 0.7 all-gather.6.cloned.1.call-update
  8.7 1.0 copy_bitcast_fusion.4
  9.7 1.0 copy_bitcast_fusion.3
  10.9 1.1 pad_maximum_fusion.1
  12.0 7.4 %all-to-all-start = ((bf16[128,16,256]{2,0,1:T(8,128)(2,1)}), bf16[128,16,256]{2,0,1:T(8,128)(2,1)S(1)}, u32[]{:S(2)}, u32[]{:S(2)}) async-start(bf16[128,16,256]{2,0,1:T(8,128)(2,1)} %pad_maximum_fusion.1), calls=%async_computation | async-start | bytes 2097152 | tf_op jit(solution)/shard_map/all_to_all | solution.py:123
  19.4 0.7 reshape.259
  20.1 40.6 %all-gather = bf16[16,1,512]{2,1,0:T(2,128)(2,1)S(1)} all-gather(bf16[1,1,512]{2,1,0:T(2,128)(2,1)S(1)} %reshape.259), channel_id=1, replica_groups=mesh['groups'=2,'fsdp'=16] {'fsdp'}, dimensions={0}, use_global_device_ids=true | all-gather | bytes 17408 | tf_op jit(solution)/shard_map/all_gather | solution.py:86
  60.9 0.5 multiply_cosine_fusion
  61.4 17.4 %all-gather.4.cloned.1.call-done = bf16[256,8192]{1,0:T(8,128)(2,1)} async-done(((bf16[256,512]{1,0:T(8,128)(2,1)}), bf16[256,8192]{1,0:T(8,128)(2,1)}) %all-gather.4.cloned.1.call-update) | async-done | bytes 4194320 | tf_op jit(solution)/shard_map/all_gather | solution.py:85
  78.9 3.1 fusion
  82.0 3.6 fusion.2
  85.6 0.5 fusion.20
  86.1 1.6 copy-done.3
  87.7 1.7 fusion.22
  89.4 1.5 pad_maximum_fusion
  91.2 7.0 %fusion.41 = f32[256,512]{1,0:T(8,128)S(1)} fusion(bf16[256,8192]{1,0:T(8,128)(2,1)} %copy-done.3, bf16[8192,512]{1,0:T(8,128)(2,1)} %param.11), kind=kOutput, calls=%fused_computation.77 | convolution fusion | flops 2147483648 | bytes 13107200 | tf_op jit(solution)/shard_map/dot_general | solution.py:117
  98.2 34.2 %all-gather.6.cloned.1.call-done = bf16[256,8192]{1,0:T(8,128)(2,1)} async-done(((bf16[256,512]{1,0:T(8,128)(2,1)}), bf16[256,8192]{1,0:T(8,128)(2,1)}) %all-gather.6.cloned.1.call-update) | async-done | bytes 4194320 | tf_op jit(solution)/shard_map/all_gather | solution.py:132
  132.4 7.0 %convolution_convert_fusion = bf16[256,512]{1,0:T(8,128)(2,1)S(1)} fusion(bf16[256,8192]{1,0:T(8,128)(2,1)} %all-gather.6.cloned.1.call-done, bf16[512,8192]{1,0:T(8,128)(2,1)} %param.14), kind=kOutput, calls=%fused_computation.24 | convolution fusion | flops 2147614720 | bytes 12845056 | tf_op jit(solution)/shard_map/dot_general | solution.py:133
  139.8 0.3 fusion.39
  140.3 4.6 %multiply_reduce_fusion = (f32[4,256]{1,0:T(4,128)S(1)}, f32[4,256,2048]{2,1,0:T(8,128)}) fusion(bf16[2048,1,256]{2,0,1:T(8,128)(2,1)S(1)} %bitcast.97, bf16[256,4,64]{2,0,1:T(8,128)(2,1)S(1)} %get-tuple-element.21, bf16[256,4,64]{2,0,1:T(8,128)(2,1)S(1)} %get-tuple-element.20), kind=kOutput, calls=%fused_computation.7 | convolution fusion | flops 541588480 | bytes 9441280 | tf_op jit(solution)/shard_map/gtd,cd->gtc/dot_general | solution.py:32
  144.8 87.2 %all-reduce.2.cloned.1.call-done = f32[256,2048]{1,0:T(8,128)} async-done(((f32[256,2048]{1,0:T(8,128)}), f32[256,2048]{1,0:T(8,128)}) %all-reduce.2.cloned.1.call-update) | async-done | bytes 2097168 | tf_op jit(solution)/shard_map/psum | solution.py:101
  232.0 1.5 slice_bitcast_fusion
  233.7 0.4 subtract_convert_fusion
  234.1 0.3 pad_maximum_fusion.2
  234.6 0.8 copy-done.4
  235.3 0.4 fusion.40
  235.9 1.9 fusion.4
  237.8 1.3 slice.63
  239.1 0.8 copy-done.5
  239.9 0.3 fusion.18
  240.3 2.3 multiply_reduce_fusion.1
  242.6 0.9 slice-done.1
  243.5 5.8 %fusion.42 = f32[256,8192]{1,0:T(8,128)} fusion(bf16[256,512]{0,1:T(8,128)(2,1)S(1)} %bitcast.107, bf16[512,8192]{1,0:T(8,128)(2,1)S(1)} %bitcast.95), kind=kOutput, calls=%fused_computation.78 | convolution fusion | flops 2147483648 | bytes 17039360 | tf_op jit(solution)/shard_map/dot_general | solution.py:143
  249.3 5.6 %convolution_bitcast_fusion = f32[2048,128]{0,1:T(8,128)} fusion(bf16[4,256,128]{1,2,0:T(8,128)(2,1)S(1)} %bitcast.108, f32[4,256,2048]{2,1,0:T(8,128)} %get-tuple-element.31, f32[4,256]{1,0:T(4,128)S(1)} %add.115, f32[4,256]{1,0:T(4,128)S(1)} %max.8), kind=kOutput, calls=%fused_computation.10 | convolution fusion | flops 545259520 | bytes 9707520 | tf_op jit(solution)/shard_map/gtc,gtd->cd/dot_general | solution.py:68
  254.9 8.5 %fusion.5 = f32[2048,128]{0,1:T(8,128)} fusion(bf16[4,256,128]{1,2,0:T(8,128)(2,1)S(1)} %bitcast.109, f32[4,256]{1,0:T(4,128)S(1)} %get-tuple-element.34, bf16[2048,1,256]{2,0,1:T(8,128)(2,1)S(1)} %bitcast.99, bf16[256,4,64]{2,0,1:T(8,128)(2,1)S(1)} %get-tuple-element.21, bf16[256,4,64]{2,0,1:T(8,128)(2,1)S(1)} %get-tuple-element.20, ...), kind=kOutput, calls=%fused_computation.12 | convolution fusion | flops 1087111168 | bytes 10760192 | tf_op jit(solution)/shard_map/gtc,gtd->cd/dot_general | solution.py:66
  263.4 3.4 copy_bitcast_fusion
  266.8 3.8 all-to-all-start.1
  270.6 0.9 constant_dynamic-slice_fusion.1
  271.5 0.7 copy.54
  272.2 0.9 constant_dynamic-slice_fusion
  273.2 0.7 copy.55
  273.9 64.4 %all-to-all-done.1 = f32[16,128,256]{1,2,0:T(8,128)S(1)} async-done(((f32[16,128,256]{1,2,0:T(8,128)}), f32[16,128,256]{1,2,0:T(8,128)S(1)}, u32[]{:S(2)}, u32[]{:S(2)}) %all-to-all-start.1) | async-done | bytes 2097184 | tf_op jit(solution)/shard_map/all_to_all | solution.py:151
  338.4 0.6 copy.80
  339.2 1.0 copy.53
  340.3 1.0 copy.52
  341.3 49.7 %reduce-scatter.2.cloned.1.call-done = f32[256,512]{1,0:T(8,128)} async-done(((f32[256,8192]{1,0:T(8,128)}), f32[256,512]{1,0:T(8,128)}) %reduce-scatter.2.cloned.1.call-update) | async-done | bytes 524304 | tf_op jit(solution)/shard_map/reduce_scatter | solution.py:144
  391.0 1.8 convert_element_type.74
  (39 shorter events, 2.1 us)
Async XLA Ops:
  7.2 78.4 %copy-start = (bf16[512,1024]{1,0:T(8,128)(2,1)S(1)}, bf16[512,1024]{1,0:T(8,128)(2,1)}, u32[]{:S(2)}) copy-start(bf16[512,1024]{1,0:T(8,128)(2,1)} %param.13) | copy-start | bytes 3145732
  7.2 71.7 %all-gather.4.cloned.1.call-start = ((), (), s32[]{:S(2)}) async-start(), calls=%async_computation.3 | async-start | bytes 4456448 | tf_op jit(solution)/shard_map/all_gather | solution.py:85
  7.9 124.5 %all-gather.6.cloned.1.call-start = ((), (), s32[]{:S(2)}) async-start(), calls=%async_computation.6 | async-start | bytes 4456448 | tf_op jit(solution)/shard_map/all_gather | solution.py:132
  12.0 128.3 %all-to-all-start = ((bf16[128,16,256]{2,0,1:T(8,128)(2,1)}), bf16[128,16,256]{2,0,1:T(8,128)(2,1)S(1)}, u32[]{:S(2)}, u32[]{:S(2)}) async-start(bf16[128,16,256]{2,0,1:T(8,128)(2,1)} %pad_maximum_fusion.1), calls=%async_computation | async-start | bytes 2097152 | tf_op jit(solution)/shard_map/all_to_all | solution.py:123
  19.4 212.6 %all-reduce.2.cloned.1.call-start = ((), (), s32[]{:S(2)}) async-start(), calls=%async_computation.4 | async-start | bytes 4194304 | tf_op jit(solution)/shard_map/psum | solution.py:101
  85.6 2.1 copy-start.3
  91.0 300.0 %reduce-scatter.2.cloned.1.call-start = ((), (), s32[]{:S(2)}) async-start(), calls=%async_computation.5 | async-start | bytes 8912896 | tf_op jit(solution)/shard_map/reduce_scatter | solution.py:144
  232.0 3.9 copy-start.2
  234.5 0.8 copy-start.4
  239.1 0.8 copy-start.5
  239.9 2.7 slice-start
  240.3 3.2 slice-start.1
  263.4 129.4 %copy-start.1 = (bf16[512,1024]{1,0:T(8,128)(2,1)S(1)}, bf16[512,1024]{1,0:T(8,128)(2,1)}, u32[]{:S(2)}) copy-start(bf16[512,1024]{1,0:T(8,128)(2,1)} %param.13) | copy-start | bytes 3145732
  266.8 71.4 %all-to-all-start.1 = ((f32[16,128,256]{1,2,0:T(8,128)}), f32[16,128,256]{1,2,0:T(8,128)S(1)}, u32[]{:S(2)}, u32[]{:S(2)}) async-start(f32[16,128,256]{1,2,0:T(8,128)} %copy_bitcast_fusion), calls=%async_computation.2 | async-start | bytes 4194304 | tf_op jit(solution)/shard_map/all_to_all | solution.py:151
Sparse Core Ops, SparseCore 0:
  10.2 68.6 all-gather.3
  81.0 51.3 all-gather.5
  136.0 95.9 all-reduce.1
  249.4 141.5 reduce-scatter.1
where the time goes:
time: 400 us; the launch traced here: 399 us
  waiting for transfers between devices  254 us (64%)
  matrix products  43.7 us (11%)
  blocking collectives  40.6 us (10%)
  other arithmetic  18.3 us (5%)
  local copies, waits for them, and re-layouts  16.8 us (4%)
  between operations  14.1 us (4%)
  starting transfers between devices  11.5 us (3%)
    psum x1, waiting for transfers between devices, on_device(): token_kv = lax.psum(partial_kv, 'fsdp')  87.2 us
    all_to_all x1, waiting for transfers between devices, on_device(): lax.all_to_all(stacked, 'fsdp', split_axis=0, concat_axis=0, tiled=True)  64.4 us
    reduce_scatter x1, waiting for transfers between devices, on_device(): lax.psum_scatter(partial_out, 'fsdp', scatter_dimension=1, tiled=True)  49.7 us
    all_gather x1, blocking collectives, on_device(): lax.all_gather(norm_gain, 'fsdp', axis=0, tiled=True)  40.6 us
    all_gather x1, waiting for transfers between devices, on_device(): cotangent = lax.all_gather(grad_out, 'fsdp', axis=1, tiled=True)  34.2 us
    all_gather x1, waiting for transfers between devices, on_device(): lax.all_gather(layer_input, 'fsdp', axis=1, tiled=True)  17.4 us
    unnamed x25, local copies, waits for them, and re-layouts  10.6 us
    dot_general x1, matrix products, head_block(): jnp.einsum('gtc,gtd->cd', grad_score, queries, preferred_element_type=jnp...  8.53 us
  transfers between devices with their start and end apart: 6, of which 5 were waited for; matrix products, arithmetic and copies ran while one was open for 15% of the time, Pallas kernels for 0%

commit v1 on v0

--- a/solution.py
+++ b/solution.py
@@ -98,7 +98,7 @@
         ],
         1,
     )
-    token_kv = lax.psum(partial_kv, "fsdp")
+    token_kv = jnp.sum(jax.lax.all_gather(partial_kv, "fsdp"), axis=0)
     positions = C + jnp.arange(token_count) % SEQ
     all_token_keys = (
         rotate(token_kv[:, :kv_width].reshape(token_count, kv_width // HD, HD), positions)

time: 400 us -> 487 us (1.22)
  waiting for transfers between devices: 254 us -> 346 us
  blocking collectives: 40.6 us -> 23.3 us
  other arithmetic: 18.3 us -> 34.5 us
    all_gather x0 -> x1, waiting for transfers between devices: none -> 149 us  [on_device(): token_kv = jnp.sum(jax.lax.all_gather(partial_kv, 'fsdp'), axis=0)]
    psum x1 -> x0, waiting for transfers between devices: 87.2 us -> none  [on_device(): token_kv = lax.psum(partial_kv, 'fsdp')]
    all_gather x1, blocking collectives: 40.6 us -> 23.3 us  [on_device(): lax.all_gather(norm_gain, 'fsdp', axis=0, tiled=True)]
    all_gather x1, waiting for transfers between devices: 17.4 us -> 33.5 us  [on_device(): lax.all_gather(layer_input, 'fsdp', axis=1, tiled=True)]
    all_gather x1, waiting for transfers between devices: 34.2 us -> 47.6 us  [on_device(): cotangent = lax.all_gather(grad_out, 'fsdp', axis=1, tiled=True)]
    reduce_sum x0 -> x1, other arithmetic: none -> 12 us  [on_device(): token_kv = jnp.sum(jax.lax.all_gather(partial_kv, 'fsdp'), axis=0)]
    unnamed x25 -> x43, local copies, waits for them, and re-layouts: 10.6 us -> 10 us
  transfers between devices with their start and end apart: 6 -> 6, of which waited for: 5 -> 5; matrix products, arithmetic and copies ran while one was open for 15% -> 12% of each run, Pallas kernels for 0% -> 0%
where the time goes in v1:
time: 487 us
  waiting for transfers between devices  346 us (71%)
  matrix products  46 us (9%)
  other arithmetic  34.5 us (7%)
  blocking collectives  23.3 us (5%)
  local copies, waits for them, and re-layouts  14.3 us (3%)
  between operations  14.2 us (3%)
  starting transfers between devices  8.51 us (2%)
    all_gather x1, waiting for transfers between devices, on_device(): token_kv = jnp.sum(jax.lax.all_gather(partial_kv, 'fsdp'), axis=0)  149 us
    all_to_all x1, waiting for transfers between devices, on_device(): lax.all_to_all(stacked, 'fsdp', split_axis=0, concat_axis=0, tiled=True)  64.6 us
    reduce_scatter x1, waiting for transfers between devices, on_device(): lax.psum_scatter(partial_out, 'fsdp', scatter_dimension=1, tiled=True)  49.7 us
    all_gather x1, waiting for transfers between devices, on_device(): cotangent = lax.all_gather(grad_out, 'fsdp', axis=1, tiled=True)  47.6 us
    all_gather x1, waiting for transfers between devices, on_device(): lax.all_gather(layer_input, 'fsdp', axis=1, tiled=True)  33.5 us
    all_gather x1, blocking collectives, on_device(): lax.all_gather(norm_gain, 'fsdp', axis=0, tiled=True)  23.3 us
    reduce_sum x1, other arithmetic, on_device(): token_kv = jnp.sum(jax.lax.all_gather(partial_kv, 'fsdp'), axis=0)  12 us
    unnamed x43, local copies, waits for them, and re-layouts  10 us
  transfers between devices with their start and end apart: 6, of which 5 were waited for; matrix products, arithmetic and copies ran while one was open for 12% of the time, Pallas kernels for 0%

profile of v1, /device:TPU:0, one launch (start us, length us, event | category | flops | bytes accessed | tf_op | source)
XLA Modules:
  0.0 486.6 jit_solution(9480537107470312706)
XLA Ops:
  7.2 0.7 all-gather.6.cloned.1.call-update
  8.0 0.7 all-gather.8.cloned.1.call-update
  8.7 0.7 reshape.260
  9.4 23.3 %all-gather.1 = bf16[16,1,512]{2,1,0:T(2,128)(2,1)S(1)} all-gather(bf16[1,1,512]{2,1,0:T(2,128)(2,1)S(1)} %reshape.260), channel_id=1, replica_groups=mesh['groups'=2,'fsdp'=16] {'fsdp'}, dimensions={0}, use_global_device_ids=true | all-gather | bytes 17408 | tf_op jit(solution)/shard_map/all_gather | solution.py:86
  32.7 33.5 %all-gather.6.cloned.1.call-done = bf16[256,8192]{1,0:T(8,128)(2,1)} async-done(((bf16[256,512]{1,0:T(8,128)(2,1)}), bf16[256,8192]{1,0:T(8,128)(2,1)}) %all-gather.6.cloned.1.call-update) | async-done | bytes 4194320 | tf_op jit(solution)/shard_map/all_gather | solution.py:85
  66.2 3.1 fusion
  69.3 3.7 fusion.2
  73.0 0.5 fusion.20
  73.5 1.5 copy-done.2
  75.0 0.4 fusion.22
  75.5 1.6 pad_maximum_fusion
  77.4 1.1 pad_maximum_fusion.1
  78.5 3.7 all-to-all-start
  82.2 0.7 fusion.19
  83.0 0.5 multiply_cosine_fusion
  83.5 47.6 %all-gather.8.cloned.1.call-done = bf16[256,8192]{1,0:T(8,128)(2,1)} async-done(((bf16[256,512]{1,0:T(8,128)(2,1)}), bf16[256,8192]{1,0:T(8,128)(2,1)}) %all-gather.8.cloned.1.call-update) | async-done | bytes 4194320 | tf_op jit(solution)/shard_map/all_gather | solution.py:132
  131.2 7.0 %convolution_convert_fusion = bf16[256,512]{1,0:T(8,128)(2,1)S(1)} fusion(bf16[256,8192]{1,0:T(8,128)(2,1)} %all-gather.8.cloned.1.call-done, bf16[512,8192]{1,0:T(8,128)(2,1)} %param.14), kind=kOutput, calls=%fused_computation.24 | convolution fusion | flops 2147614720 | bytes 12845056 | tf_op jit(solution)/shard_map/dot_general | solution.py:133
  138.2 0.8 copy.44
  139.0 8.3 %fusion.41 = f32[256,512]{1,0:T(8,128)S(1)} fusion(bf16[256,8192]{1,0:T(8,128)(2,1)} %copy-done.2, bf16[8192,512]{1,0:T(8,128)(2,1)} %param.11), kind=kOutput, calls=%fused_computation.76 | convolution fusion | flops 2147483648 | bytes 13107200 | tf_op jit(solution)/shard_map/dot_general | solution.py:117
  147.4 0.2 reshape.247
  147.5 0.3 fusion.39
  148.1 4.5 multiply_reduce_fusion
  152.6 148.9 %all-gather.10.cloned.1.call-done = f32[4096,2048]{1,0:T(8,128)} async-done(((f32[256,2048]{1,0:T(8,128)}), f32[4096,2048]{1,0:T(8,128)}) %all-gather.10.cloned.1.call-update) | async-done | bytes 33554448 | tf_op jit(solution)/shard_map/all_gather | solution.py:101
  301.5 12.0 %reduce_sum.55 = f32[256,2048]{1,0:T(8,128)S(1)} reduce(f32[16,256,2048]{2,1,0:T(8,128)} %bitcast.94, f32[]{:T(128)} %constant.68.clone.1), dimensions={0}, to_apply=%region_2.3 | reduce | flops 7864320 | bytes 35651588 | tf_op jit(solution)/shard_map/reduce_sum | solution.py:101
  313.6 1.0 slice_bitcast_fusion
  314.7 1.0 copy.62
  315.7 1.4 copy.66
  317.1 1.4 subtract_convert_fusion
  318.5 0.3 pad_maximum_fusion.2
  318.9 0.8 copy-done.9
  319.7 1.9 fusion.40
  321.8 4.4 fusion.4
  326.2 1.3 fusion.18
  327.6 2.3 multiply_reduce_fusion.1
  330.0 5.8 %fusion.42 = f32[256,8192]{1,0:T(8,128)} fusion(bf16[256,512]{0,1:T(8,128)(2,1)S(1)} %bitcast.111, bf16[512,8192]{1,0:T(8,128)(2,1)S(1)} %bitcast.99), kind=kOutput, calls=%fused_computation.77 | convolution fusion | flops 2147483648 | bytes 17039360 | tf_op jit(solution)/shard_map/dot_general | solution.py:143
  335.8 5.6 %convolution_bitcast_fusion = f32[2048,128]{0,1:T(8,128)} fusion(bf16[4,256,128]{1,2,0:T(8,128)(2,1)S(1)} %bitcast.112, f32[4,256,2048]{2,1,0:T(8,128)} %get-tuple-element.31, f32[4,256]{1,0:T(4,128)S(1)} %add.113, f32[4,256]{1,0:T(4,128)S(1)} %max.8), kind=kOutput, calls=%fused_computation.10 | convolution fusion | flops 545259520 | bytes 9707520 | tf_op jit(solution)/shard_map/gtc,gtd->cd/dot_general | solution.py:68
  341.4 8.3 %fusion.5 = f32[2048,128]{0,1:T(8,128)} fusion(bf16[4,256,128]{1,2,0:T(8,128)(2,1)S(1)} %bitcast.113, f32[4,256]{1,0:T(4,128)S(1)} %get-tuple-element.34, bf16[2048,1,256]{2,0,1:T(8,128)(2,1)S(1)} %bitcast.103, bf16[256,4,64]{2,0,1:T(8,128)(2,1)S(1)} %copy-done.4, bf16[256,4,64]{2,0,1:T(8,128)(2,1)S(1)} %get-tuple-element.20, ...), kind=kOutput, calls=%fused_computation.12 | convolution fusion | flops 1087111168 | bytes 10760192 | tf_op jit(solution)/shard_map/gtc,gtd->cd/dot_general | solution.py:66
  349.7 3.5 copy_bitcast_fusion
  353.2 4.7 all-to-all-start.1
  357.9 0.9 constant_dynamic-slice_fusion.1
  358.9 0.7 copy.53
  359.6 1.4 constant_dynamic-slice_fusion
  360.9 64.6 %all-to-all-done.1 = f32[16,128,256]{1,2,0:T(8,128)S(1)} async-done(((f32[16,128,256]{1,2,0:T(8,128)}), f32[16,128,256]{1,2,0:T(8,128)S(1)}, u32[]{:S(2)}, u32[]{:S(2)}) %all-to-all-start.1) | async-done | bytes 2097184 | tf_op jit(solution)/shard_map/all_to_all | solution.py:151
  425.7 0.6 copy.77
  426.5 1.0 copy.52
  427.6 1.0 copy.51
  428.6 49.7 %reduce-scatter.2.cloned.1.call-done = f32[256,512]{1,0:T(8,128)} async-done(((f32[256,8192]{1,0:T(8,128)}), f32[256,512]{1,0:T(8,128)}) %reduce-scatter.2.cloned.1.call-update) | async-done | bytes 524304 | tf_op jit(solution)/shard_map/reduce_scatter | solution.py:144
  478.3 1.8 convert_element_type.74
  (59 shorter events, 1.6 us)
Async XLA Ops:
  7.2 65.9 %copy-start = (bf16[512,1024]{1,0:T(8,128)(2,1)S(1)}, bf16[512,1024]{1,0:T(8,128)(2,1)}, u32[]{:S(2)}) copy-start(bf16[512,1024]{1,0:T(8,128)(2,1)} %param.13) | copy-start | bytes 3145732
  7.2 67.8 %copy-start.8 = (bf16[512,1024]{1,0:T(8,128)(2,1)S(1)}, bf16[512,1024]{1,0:T(8,128)(2,1)}, u32[]{:S(2)}) copy-start(bf16[512,1024]{1,0:T(8,128)(2,1)} %param.12) | copy-start | bytes 3145732
  7.2 59.0 %all-gather.6.cloned.1.call-start = ((), (), s32[]{:S(2)}) async-start(), calls=%async_computation.3 | async-start | bytes 4456448 | tf_op jit(solution)/shard_map/all_gather | solution.py:85
  7.9 123.2 %all-gather.8.cloned.1.call-start = ((), (), s32[]{:S(2)}) async-start(), calls=%async_computation.5 | async-start | bytes 4456448 | tf_op jit(solution)/shard_map/all_gather | solution.py:132
  8.7 292.8 %all-gather.10.cloned.1.call-start = ((), (), s32[]{:S(2)}) async-start(), calls=%async_computation.6 | async-start | bytes 35651584 | tf_op jit(solution)/shard_map/all_gather | solution.py:101
  69.3 7.7 %copy-start.10 = (bf16[128,1024]{1,0:T(8,128)(2,1)S(1)}, bf16[128,1024]{1,0:T(8,128)(2,1)}, u32[]{:S(2)}) copy-start(bf16[128,1024]{1,0:T(8,128)(2,1)} %param.15) | copy-start | bytes 786436
  69.3 7.8 %copy-start.11 = (bf16[128,1024]{1,0:T(8,128)(2,1)S(1)}, bf16[128,1024]{1,0:T(8,128)(2,1)}, u32[]{:S(2)}) copy-start(bf16[128,1024]{1,0:T(8,128)(2,1)} %param.16) | copy-start | bytes 786436
  73.0 2.0 copy-start.2
  78.5 69.6 %all-to-all-start = ((bf16[128,16,256]{2,0,1:T(8,128)(2,1)}), bf16[128,16,256]{2,0,1:T(8,128)(2,1)S(1)}, u32[]{:S(2)}, u32[]{:S(2)}) async-start(bf16[128,16,256]{2,0,1:T(8,128)(2,1)} %pad_maximum_fusion.1), calls=%async_computation | async-start | bytes 2097152 | tf_op jit(solution)/shard_map/all_to_all | solution.py:123
  82.2 396.1 %reduce-scatter.2.cloned.1.call-start = ((), (), s32[]{:S(2)}) async-start(), calls=%async_computation.4 | async-start | bytes 8912896 | tf_op jit(solution)/shard_map/reduce_scatter | solution.py:144
  83.5 64.4 %copy-start.7 = (f32[256,64]{1,0:T(8,128)}, f32[256,64]{1,0:T(8,128)S(1)}, u32[]{:S(2)}) copy-start(f32[256,64]{1,0:T(8,128)S(1)} %get-tuple-element.29) | copy-start | bytes 196612
  148.0 165.5 %copy-start.3 = (bf16[256,4,64]{2,0,1:T(8,128)(2,1)}, bf16[256,4,64]{2,0,1:T(8,128)(2,1)S(1)}, u32[]{:S(2)}) copy-start(bf16[256,4,64]{2,0,1:T(8,128)(2,1)S(1)} %get-tuple-element.21) | copy-start | bytes 393220
  148.1 153.5 %copy-start.5 = (bf16[128,16,256]{2,0,1:T(8,128)(2,1)}, bf16[128,16,256]{2,0,1:T(8,128)(2,1)S(1)}, u32[]{:S(2)}) copy-start(bf16[128,16,256]{2,0,1:T(8,128)(2,1)S(1)} %all-to-all-done) | copy-start | bytes 3145732
  314.7 5.0 %copy-start.4 = (bf16[256,4,64]{2,0,1:T(8,128)(2,1)S(1)}, bf16[256,4,64]{2,0,1:T(8,128)(2,1)}, u32[]{:S(2)}) copy-start(bf16[256,4,64]{2,0,1:T(8,128)(2,1)} %copy-done.3) | copy-start | bytes 393220
  318.8 8.8 %slice-start = ((s8[8388608]{0:T(1024)(128)(4,1)}), s8[4194304]{0:T(1024)(128)(4,1)S(1)}, s32[]{:S(2)}) async-start(s8[8388608]{0:T(1024)(128)(4,1)} %bitcast.95), calls=%async_computation.7 | async-start | bytes 8388608
  318.8 8.8 %copy-start.6 = (bf16[128,16,256]{2,0,1:T(8,128)(2,1)S(1)}, bf16[128,16,256]{2,0,1:T(8,128)(2,1)}, u32[]{:S(2)}) copy-start(bf16[128,16,256]{2,0,1:T(8,128)(2,1)} %copy-done.5) | copy-start | bytes 3145732
  318.8 8.8 %copy-start.12 = (bf16[256,512]{0,1:T(8,128)(2,1)S(1)}, bf16[256,512]{0,1:T(8,128)(2,1)}, u32[]{:S(2)}) copy-start(bf16[256,512]{0,1:T(8,128)(2,1)} %copy.44) | copy-start | bytes 786436
  318.9 0.8 copy-start.9
  321.8 5.8 %slice-start.1 = ((s8[8388608]{0:T(1024)(128)(4,1)}), s8[4194304]{0:T(1024)(128)(4,1)S(1)}, s32[]{:S(2)}) async-start(s8[8388608]{0:T(1024)(128)(4,1)} %bitcast.95), calls=%async_computation.8 | async-start | bytes 8388608
  326.2 3.7 slice-start.2
  327.6 2.4 slice-start.3
  349.7 130.3 %copy-start.1 = (bf16[512,1024]{1,0:T(8,128)(2,1)S(1)}, bf16[512,1024]{1,0:T(8,128)(2,1)}, u32[]{:S(2)}) copy-start(bf16[512,1024]{1,0:T(8,128)(2,1)} %param.13) | copy-start | bytes 3145732
  353.2 72.4 %all-to-all-start.1 = ((f32[16,128,256]{1,2,0:T(8,128)}), f32[16,128,256]{1,2,0:T(8,128)S(1)}, u32[]{:S(2)}, u32[]{:S(2)}) async-start(f32[16,128,256]{1,2,0:T(8,128)} %copy_bitcast_fusion), calls=%async_computation.2 | async-start | bytes 4194304 | tf_op jit(solution)/shard_map/all_to_all | solution.py:151
Sparse Core Ops, SparseCore 0:
  10.2 55.9 all-gather.5
  68.4 62.7 all-gather.7
  132.8 168.7 all-gather.9
  335.9 142.3 reduce-scatter.1
